TPU v7x, 256 devices: a whole 4x4x8 slice. The times are simulated.
256 devices in a mesh: dev: 8 (over z), ha: 4 (over y), wa: 8 (over x, core).
Axes of the slice: x: 4, y: 4, z: 8, core: 2. Of those that a mesh axis runs over, the one named last changes fastest.
Arguments:
- volume: float32 [32, 32, 64, 256], P('dev', 'ha', 'wa'), may hold values from -6 to 6
- kernel: float32 [256, 27, 256], replicated, may hold values from -0.078125 to 0.078125
- upstream: float32 [32, 32, 64, 256], P('dev', 'ha', 'wa'), may hold values from -6 to 6
Outputs:
- output: float32 [32, 32, 64, 256], P('dev', 'ha', 'wa')
- volume_grad: float32 [32, 32, 64, 256], P('dev', 'ha', 'wa')
- kernel_grad: float32 [256, 27, 256], P('wa')
All inputs are finite; a program needn't handle non-finite values.
Results may differ from a plain program's by a relative error of at most 0.0001.
Values sent between devices are 32-bit elements; how exact they have to be, the bound alone decides.
A program may use at most 128 MiB of HBM per device.

v0:
```python
import math
import jax
import jax.numpy as jnp
from jax import lax
from jax.sharding import PartitionSpec as P


def padded_2(shard, sides, width):
    for axis, dim in sides:
        count, length = (lax.axis_size(axis), shard.shape[dim])
        up = [(i, (i + 1) % count) for i in range(count)]
        down = [(j, i) for i, j in up]
        last = lax.slice_in_dim(shard, length - width, length, axis=dim)
        initial = lax.slice_in_dim(shard, 0, width, axis=dim)
        before = lax.ppermute(last, axis, up)
        after = lax.ppermute(initial, axis, down)
        shard = jnp.concatenate([before, shard, after], axis=dim)
    return shard


def tap_offsets():
    return [(da, db, dc) for da in (-1, 0, 1) for db in (-1, 0, 1) for dc in (-1, 0, 1)]


def per_device(volume, kernel, upstream):
    depth_cells, height_cells, width_cells, channels = volume.shape
    cells = depth_cells * height_cells * width_cells
    stacked = jnp.stack([volume, upstream])
    padded = padded_2(stacked, (("dev", 1), ("ha", 2), ("wa", 3)), 1)
    forward_windows = []
    backward_windows = []
    for da, db, dc in tap_offsets():
        forward_windows.append(
            padded[
                0,
                1 + da : 1 + da + depth_cells,
                1 + db : 1 + db + height_cells,
                1 + dc : 1 + dc + width_cells,
            ].reshape(cells, channels)
        )
        backward_windows.append(
            padded[
                1,
                1 - da : 1 - da + depth_cells,
                1 - db : 1 - db + height_cells,
                1 - dc : 1 - dc + width_cells,
            ].reshape(cells, channels)
        )
    forward_patches = jnp.stack(forward_windows, axis=1)
    backward_patches = jnp.stack(backward_windows, axis=1)
    output = jnp.einsum(
        "ntc,cto->no",
        forward_patches,
        kernel,
        precision=lax.Precision.HIGHEST,
        preferred_element_type=jnp.float32,
    )
    volume_grad = jnp.einsum(
        "nto,cto->nc",
        backward_patches,
        kernel,
        precision=lax.Precision.HIGHEST,
        preferred_element_type=jnp.float32,
    )
    flat_up = upstream.reshape(cells, channels)
    total_cells = cells * lax.axis_size("dev") * lax.axis_size("ha") * lax.axis_size("wa")
    factor = 1.0 / math.sqrt(total_cells)
    owned = channels // lax.axis_size("wa")
    summed = lax.psum(
        jnp.einsum(
            "ntc,no->cto",
            forward_patches,
            flat_up,
            precision=lax.Precision.HIGHEST,
            preferred_element_type=jnp.float32,
        )
        * factor,
        ("dev", "ha", "wa"),
    )
    kernel_grad = lax.dynamic_slice_in_dim(summed, lax.axis_index("wa") * owned, owned, 0)
    return (output.reshape(volume.shape), volume_grad.reshape(volume.shape), kernel_grad)


def solution(mesh):
    placed = (P("dev", "ha", "wa", None), P(), P("dev", "ha", "wa", None))
    return jax.shard_map(
        per_device,
        mesh=mesh,
        in_specs=placed,
        out_specs=(P("dev", "ha", "wa", None), P("dev", "ha", "wa", None), P("wa", None, None)),
        check_vma=False,
    )
```

profile of v0, /device:TPU:2, one launch (start us, length us, event | category | flops | bytes accessed | tf_op | source)
XLA Modules:
  0.0 338.1 jit_solution(18164718943896220300)
XLA Ops:
  7.2 1.0 pad_maximum_fusion.9
  8.2 2.0 collective-permute-start
  10.2 4.0 %collective-permute-start.1 = (f32[2,1,8,8,256]{4,3,2,1,0:T(8,128)S(1)}, f32[2,1,8,8,256]{4,3,2,1,0:T(8,128)S(1)}, u32[]{:S(2)}, u32[]{:S(2)}) collective-permute-start(f32[2,1,8,8,256]{4,3,2,1,0:T(8,128)S(1)} %get-tuple-element.66), channel_id=1, source_target_pairs={{32,0},{64,32},{96,64},{128,96},{160,128},{192,160},{224,192},{0,2... | collective-permute-start | bytes 393224 | tf_op jit(solution)/shard_map/ppermute | solution.py:16
  14.3 3.4 %collective-permute-done = f32[2,1,8,8,256]{4,3,2,1,0:T(8,128)S(1)} collective-permute-done((f32[2,1,8,8,256]{4,3,2,1,0:T(8,128)S(1)}, f32[2,1,8,8,256]{4,3,2,1,0:T(8,128)S(1)}, u32[]{:S(2)}, u32[]{:S(2)}) %collective-permute-start) | collective-permute-done | bytes 131104 | tf_op jit(solution)/shard_map/ppermute | solution.py:15
  17.7 0.8 pad_maximum_fusion.19
  18.5 1.7 collective-permute-start.2
  20.2 1.7 collective-permute-start.3
  21.9 2.0 pad_maximum_fusion.2
  24.8 1.4 pad_maximum_fusion.10
  26.2 1.7 collective-permute-start.5
  27.9 1.4 pad_maximum_fusion.1
  29.3 1.3 fusion.2
  30.6 0.6 pad_maximum_fusion
  31.3 1.5 fusion.1
  32.7 0.7 constant_dynamic-update-slice_fusion.53
  33.5 1.5 fusion
  35.7 2.8 copy-done
  38.5 13.7 %multiply_bitcast_fusion = f32[256,27,256]{2,0,1:T(8,128)} fusion(f32[256,27,256]{2,0,1:T(8,128)S(1)} %constant_dynamic-update-slice_fusion, f32[256,256,1]{1,0,2:T(8,128)S(1)} %bitcast.83), kind=kOutput, calls=%fused_computation | convolution fusion | flops 5437587456 | bytes 14417920 | tf_op jit(solution)/shard_map/ntc,no->cto/dot_general | solution.py:70
  52.3 1.8 constant_dynamic-update-slice_fusion.52
  54.1 1.7 constant_dynamic-update-slice_fusion.51
  55.8 1.7 constant_dynamic-update-slice_fusion.50
  57.5 1.7 constant_dynamic-update-slice_fusion.49
  59.1 1.7 constant_dynamic-update-slice_fusion.48
  60.8 1.7 constant_dynamic-update-slice_fusion.47
  62.5 1.8 constant_dynamic-update-slice_fusion.46
  64.3 1.7 constant_dynamic-update-slice_fusion.45
  66.0 1.7 constant_dynamic-update-slice_fusion.44
  67.7 1.7 constant_dynamic-update-slice_fusion.43
  69.3 1.7 constant_dynamic-update-slice_fusion.42
  71.0 1.7 constant_dynamic-update-slice_fusion.41
  72.7 0.7 constant_dynamic-update-slice_fusion.40
  73.5 1.7 constant_dynamic-update-slice_fusion.39
  75.1 0.7 constant_dynamic-update-slice_fusion.38
  75.9 0.7 constant_dynamic-update-slice_fusion.37
  76.6 0.7 constant_dynamic-update-slice_fusion.36
  77.3 0.7 constant_dynamic-update-slice_fusion.35
  78.1 0.7 constant_dynamic-update-slice_fusion.34
  78.8 0.7 constant_dynamic-update-slice_fusion.33
  79.5 0.7 constant_dynamic-update-slice_fusion.32
  80.2 0.7 constant_dynamic-update-slice_fusion.31
  81.0 0.7 constant_dynamic-update-slice_fusion.30
  81.7 0.7 constant_dynamic-update-slice_fusion.29
  82.4 0.7 constant_dynamic-update-slice_fusion.28
  83.1 0.7 constant_dynamic-update-slice_fusion.27
  83.9 14.6 %fusion.4 = f32[256,256,1]{1,0,2:T(8,128)} fusion(f32[256,27,256]{2,0,1:T(8,128)S(1)} %bitcast.74, f32[256,27,256]{2,0,1:T(8,128)} %param.4), kind=kOutput, calls=%fused_computation.82 | convolution fusion | flops 5435817984 | bytes 14417920 | tf_op jit(solution)/shard_map/ntc,cto->no/dot_general | solution.py:51
  98.5 6.5 %fusion.5 = f32[256,256,1]{1,0,2:T(8,128)} fusion(f32[256,27,256]{2,0,1:T(8,128)S(1)} %copy-done.3, f32[256,27,256]{2,0,1:T(8,128)S(1)} %bitcast.76), kind=kOutput, calls=%fused_computation.83 | convolution fusion | flops 5435817984 | bytes 14417920 | tf_op jit(solution)/shard_map/nto,cto->nc/dot_general | solution.py:58
  105.1 224.1 %all-reduce.2.cloned.1.call-done = f32[256,27,256]{2,0,1:T(8,128)} async-done(((f32[256,27,256]{2,0,1:T(8,128)}), f32[256,27,256]{2,0,1:T(8,128)}) %all-reduce.2.cloned.1.call-update) | async-done | bytes 7077904 | tf_op jit(solution)/shard_map/psum | solution.py:69
  329.1 2.2 constant_dynamic-slice_fusion
  (74 shorter events, 1.6 us)
Async XLA Ops:
  7.2 23.5 %copy-start.2 = (f32[4,8,8,256]{3,2,1,0:T(8,128)S(1)}, f32[4,8,8,256]{3,2,1,0:T(8,128)}, u32[]{:S(2)}) copy-start(f32[4,8,8,256]{3,2,1,0:T(8,128)} %param.3) | copy-start | bytes 786436
  7.2 23.4 %copy-start.1 = (f32[4,8,8,256]{3,2,1,0:T(8,128)S(1)}, f32[4,8,8,256]{3,2,1,0:T(8,128)}, u32[]{:S(2)}) copy-start(f32[4,8,8,256]{3,2,1,0:T(8,128)} %param.5) | copy-start | bytes 786436
  7.2 321.9 %all-reduce.2.cloned.1.call-start = ((), (), s32[]{:S(2)}) async-start(), calls=%async_computation | async-start | bytes 14155776 | tf_op jit(solution)/shard_map/psum | solution.py:69
  8.2 9.4 %collective-permute-start = (f32[2,1,8,8,256]{4,3,2,1,0:T(8,128)S(1)}, f32[2,1,8,8,256]{4,3,2,1,0:T(8,128)S(1)}, u32[]{:S(2)}, u32[]{:S(2)}) collective-permute-start(f32[2,1,8,8,256]{4,3,2,1,0:T(8,128)S(1)} %get-tuple-element.65), channel_id=1, source_target_pairs={{0,32},{32,64},{64,96},{96,128},{128,160},{160,192},{192,224},{224... | collective-permute-start | bytes 393224 | tf_op jit(solution)/shard_map/ppermute | solution.py:15
  10.2 7.4 %collective-permute-start.1 = (f32[2,1,8,8,256]{4,3,2,1,0:T(8,128)S(1)}, f32[2,1,8,8,256]{4,3,2,1,0:T(8,128)S(1)}, u32[]{:S(2)}, u32[]{:S(2)}) collective-permute-start(f32[2,1,8,8,256]{4,3,2,1,0:T(8,128)S(1)} %get-tuple-element.66), channel_id=1, source_target_pairs={{32,0},{64,32},{96,64},{128,96},{160,128},{192,160},{224,192},{0,2... | collective-permute-start | bytes 393224 | tf_op jit(solution)/shard_map/ppermute | solution.py:16
  18.5 5.9 %collective-permute-start.2 = (f32[2,6,1,8,256]{4,3,2,1,0:T(8,128)S(1)}, f32[2,6,1,8,256]{4,3,2,1,0:T(8,128)S(1)}, u32[]{:S(2)}, u32[]{:S(2)}) collective-permute-start(f32[2,6,1,8,256]{4,3,2,1,0:T(8,128)S(1)} %get-tuple-element.57), channel_id=1, source_target_pairs={{0,8},{8,16},{16,24},{24,0},{1,9},{9,17},{17,25},{25,1},{2,10},{10... | collective-permute-start | bytes 294920 | tf_op jit(solution)/shard_map/ppermute | solution.py:15
  20.2 4.6 %collective-permute-start.3 = (f32[2,6,1,8,256]{4,3,2,1,0:T(8,128)S(1)}, f32[2,6,1,8,256]{4,3,2,1,0:T(8,128)S(1)}, u32[]{:S(2)}, u32[]{:S(2)}) collective-permute-start(f32[2,6,1,8,256]{4,3,2,1,0:T(8,128)S(1)} %get-tuple-element.58), channel_id=1, source_target_pairs={{8,0},{16,8},{24,16},{0,24},{9,1},{17,9},{25,17},{1,25},{10,2},{18... | collective-permute-start | bytes 294920 | tf_op jit(solution)/shard_map/ppermute | solution.py:16
  26.2 4.4 %collective-permute-start.4 = (f32[2,6,10,1,256]{4,3,2,1,0:T(1,128)S(1)}, f32[2,6,10,1,256]{4,3,2,1,0:T(1,128)S(1)}, u32[]{:S(2)}, u32[]{:S(2)}) collective-permute-start(f32[2,6,10,1,256]{4,3,2,1,0:T(1,128)S(1)} %get-tuple-element.42), channel_id=1, source_target_pairs={{0,1},{1,2},{2,3},{3,4},{4,5},{5,6},{6,7},{7,0},{8,9},{9,10},{10,1... | collective-permute-start | bytes 368648 | tf_op jit(solution)/shard_map/ppermute | solution.py:15
  26.2 4.4 %collective-permute-start.5 = (f32[2,6,10,1,256]{4,3,2,1,0:T(1,128)S(1)}, f32[2,6,10,1,256]{4,3,2,1,0:T(1,128)S(1)}, u32[]{:S(2)}, u32[]{:S(2)}) collective-permute-start(f32[2,6,10,1,256]{4,3,2,1,0:T(1,128)S(1)} %get-tuple-element.41), channel_id=1, source_target_pairs={{1,0},{2,1},{3,2},{4,3},{5,4},{6,5},{7,6},{0,7},{9,8},{10,9},{11,1... | collective-permute-start | bytes 368648 | tf_op jit(solution)/shard_map/ppermute | solution.py:16
  35.7 2.8 copy-start
  52.2 31.7 %slice-start = ((s8[7077888]{0:T(1024)(128)(4,1)}), s8[2883584]{0:T(1024)(128)(4,1)S(1)}, s32[]{:S(2)}) async-start(s8[7077888]{0:T(1024)(128)(4,1)} %bitcast.73), calls=%async_computation.1 | async-start | bytes 5767168
  52.2 22.9 %copy-start.11 = (f32[1,4,8,8,256]{4,3,2,1,0:T(8,128)S(1)}, f32[1,4,8,8,256]{4,3,2,1,0:T(8,128)}, u32[]{:S(2)}) copy-start(f32[1,4,8,8,256]{4,3,2,1,0:T(8,128)} %get-tuple-element.24) | copy-start | bytes 786436
  52.2 23.7 %copy-start.6 = (f32[1,4,8,8,256]{4,3,2,1,0:T(8,128)S(1)}, f32[1,4,8,8,256]{4,3,2,1,0:T(8,128)}, u32[]{:S(2)}) copy-start(f32[1,4,8,8,256]{4,3,2,1,0:T(8,128)} %get-tuple-element.44) | copy-start | bytes 786436
  52.2 24.4 %copy-start.14 = (f32[1,4,8,8,256]{4,3,2,1,0:T(8,128)S(1)}, f32[1,4,8,8,256]{4,3,2,1,0:T(8,128)}, u32[]{:S(2)}) copy-start(f32[1,4,8,8,256]{4,3,2,1,0:T(8,128)} %get-tuple-element.6) | copy-start | bytes 786436
  52.2 25.1 %copy-start.10 = (f32[1,4,8,8,256]{4,3,2,1,0:T(8,128)S(1)}, f32[1,4,8,8,256]{4,3,2,1,0:T(8,128)}, u32[]{:S(2)}) copy-start(f32[1,4,8,8,256]{4,3,2,1,0:T(8,128)} %get-tuple-element.23) | copy-start | bytes 786436
  52.2 25.8 %copy-start.5 = (f32[1,4,8,8,256]{4,3,2,1,0:T(8,128)S(1)}, f32[1,4,8,8,256]{4,3,2,1,0:T(8,128)}, u32[]{:S(2)}) copy-start(f32[1,4,8,8,256]{4,3,2,1,0:T(8,128)} %get-tuple-element.72) | copy-start | bytes 786436
  52.3 26.5 %copy-start.13 = (f32[1,4,8,8,256]{4,3,2,1,0:T(8,128)S(1)}, f32[1,4,8,8,256]{4,3,2,1,0:T(8,128)}, u32[]{:S(2)}) copy-start(f32[1,4,8,8,256]{4,3,2,1,0:T(8,128)} %get-tuple-element.5) | copy-start | bytes 786436
  52.3 27.2 %copy-start.8 = (f32[1,4,8,8,256]{4,3,2,1,0:T(8,128)S(1)}, f32[1,4,8,8,256]{4,3,2,1,0:T(8,128)}, u32[]{:S(2)}) copy-start(f32[1,4,8,8,256]{4,3,2,1,0:T(8,128)} %get-tuple-element.22) | copy-start | bytes 786436
  52.3 28.7 %copy-start.12 = (f32[1,4,8,8,256]{4,3,2,1,0:T(8,128)S(1)}, f32[1,4,8,8,256]{4,3,2,1,0:T(8,128)}, u32[]{:S(2)}) copy-start(f32[1,4,8,8,256]{4,3,2,1,0:T(8,128)} %get-tuple-element.4) | copy-start | bytes 786436
  52.3 29.4 %copy-start.7 = (f32[1,4,8,8,256]{4,3,2,1,0:T(8,128)S(1)}, f32[1,4,8,8,256]{4,3,2,1,0:T(8,128)}, u32[]{:S(2)}) copy-start(f32[1,4,8,8,256]{4,3,2,1,0:T(8,128)} %get-tuple-element.21) | copy-start | bytes 786436
  52.3 30.1 %copy-start.4 = (f32[1,4,8,8,256]{4,3,2,1,0:T(8,128)S(1)}, f32[1,4,8,8,256]{4,3,2,1,0:T(8,128)}, u32[]{:S(2)}) copy-start(f32[1,4,8,8,256]{4,3,2,1,0:T(8,128)} %get-tuple-element.43) | copy-start | bytes 786436
  52.3 30.8 %copy-start.9 = (f32[1,4,8,8,256]{4,3,2,1,0:T(8,128)S(1)}, f32[1,4,8,8,256]{4,3,2,1,0:T(8,128)}, u32[]{:S(2)}) copy-start(f32[1,4,8,8,256]{4,3,2,1,0:T(8,128)} %get-tuple-element.3) | copy-start | bytes 786436
  62.5 21.4 %slice-start.1 = ((s8[7077888]{0:T(1024)(128)(4,1)}), s8[4194304]{0:T(1024)(128)(4,1)S(1)}, s32[]{:S(2)}) async-start(s8[7077888]{0:T(1024)(128)(4,1)} %bitcast.73), calls=%async_computation.2 | async-start | bytes 8388608
  82.4 16.1 %slice-start.2 = ((s8[7077888]{0:T(1024)(128)(4,1)}), s8[4194304]{0:T(1024)(128)(4,1)S(1)}, s32[]{:S(2)}) async-start(s8[7077888]{0:T(1024)(128)(4,1)} %bitcast.75), calls=%async_computation.3 | async-start | bytes 8388608
  83.9 14.7 %slice-start.3 = ((s8[7077888]{0:T(1024)(128)(4,1)}), s8[2883584]{0:T(1024)(128)(4,1)S(1)}, s32[]{:S(2)}) async-start(s8[7077888]{0:T(1024)(128)(4,1)} %bitcast.75), calls=%async_computation.4 | async-start | bytes 5767168
  83.9 14.7 %copy-start.3 = (f32[256,27,256]{2,0,1:T(8,128)S(1)}, f32[256,27,256]{2,0,1:T(8,128)}, u32[]{:S(2)}) copy-start(f32[256,27,256]{2,0,1:T(8,128)} %constant_dynamic-update-slice_fusion.27) | copy-start | bytes 21233668
Sparse Core Ops, SparseCore 0:
  52.3 276.7 all-reduce.1
where the time goes:
time: 339 us; the launch traced here: 338 us
  waiting for transfers between devices  228 us (67%)
  local copies, waits for them, and re-layouts  42.1 us (12%)
  matrix products  34.9 us (10%)
  between operations  14.4 us (4%)
  starting transfers between devices  11.2 us (3%)
  other arithmetic  7.22 us (2%)
    psum x1, waiting for transfers between devices, per_device(): lax.psum(jnp.einsum('ntc,no->cto', forward_patches, flat_up, precision=la...  224 us
    unnamed x90, local copies, waits for them, and re-layouts  34.9 us
    dot_general x1, matrix products, per_device(): jnp.einsum('ntc,cto->no', forward_patches, kernel, precision=lax.Precisio...  14.6 us
    dot_general x1, matrix products, per_device(): jnp.einsum('ntc,no->cto', forward_patches, flat_up, precision=lax.Precisi...  13.7 us
    ppermute x3, starting transfers between devices, padded_2(): after = lax.ppermute(initial, axis, down)  7.47 us
  transfers between devices with their start and end apart: 7, of which 4 were waited for; matrix products, arithmetic and copies ran while one was open for 17% of the time, Pallas kernels for 0%

commit v1 on v0

--- a/solution.py
+++ b/solution.py
@@ -67,15 +67,18 @@
     factor = 1.0 / math.sqrt(total_cells)
     owned = channels // lax.axis_size("wa")
     summed = lax.psum(
-        jnp.einsum(
-            "ntc,no->cto",
-            forward_patches,
-            flat_up,
-            precision=lax.Precision.HIGHEST,
-            preferred_element_type=jnp.float32,
-        )
-        * factor,
-        ("dev", "ha", "wa"),
+        lax.psum(
+            jnp.einsum(
+                "ntc,no->cto",
+                forward_patches,
+                flat_up,
+                precision=lax.Precision.HIGHEST,
+                preferred_element_type=jnp.float32,
+            )
+            * factor,
+            "dev",
+        ),
+        ("ha", "wa"),
     )
     kernel_grad = lax.dynamic_slice_in_dim(summed, lax.axis_index("wa") * owned, owned, 0)
     return (output.reshape(volume.shape), volume_grad.reshape(volume.shape), kernel_grad)

time: 339 us -> 356 us (1.050)
  matrix products: 34.9 us -> 45.1 us
  waiting for transfers between devices: 228 us -> 235 us
    psum x0 -> x1, waiting for transfers between devices: none -> 70.5 us  [per_device(): lax.psum(lax.psum(jnp.einsum('ntc,no->cto', forward_patches, flat_up, pre...]
    psum x1, waiting for transfers between devices: 224 us -> 159 us  [per_device(): lax.psum(jnp.einsum('ntc,no->cto', forward_patches, flat_up, precision=la...]
    dot_general x1, matrix products: 6.54 us -> 17 us  [per_device(): jnp.einsum('nto,cto->nc', backward_patches, kernel, precision=lax.Precisi...]
    unnamed x90 -> x76, local copies, waits for them, and re-layouts: 34.9 us -> 35.1 us
  transfers between devices with their start and end apart: 7 -> 8, of which waited for: 4 -> 5; matrix products, arithmetic and copies ran while one was open for 17% -> 19% of each run, Pallas kernels for 0% -> 0%
where the time goes in v1:
time: 356 us; the launch traced here: 354 us
  waiting for transfers between devices  235 us (66%)
  matrix products  45.1 us (13%)
  local copies, waits for them, and re-layouts  41.8 us (12%)
  between operations  14.4 us (4%)
  starting transfers between devices  11.2 us (3%)
  other arithmetic  6.52 us (2%)
    psum x1, waiting for transfers between devices, per_device(): lax.psum(jnp.einsum('ntc,no->cto', forward_patches, flat_up, precision=la...  159 us
    psum x1, waiting for transfers between devices, per_device(): lax.psum(lax.psum(jnp.einsum('ntc,no->cto', forward_patches, flat_up, pre...  70.5 us
    unnamed x76, local copies, waits for them, and re-layouts  35.1 us
    dot_general x1, matrix products, per_device(): jnp.einsum('nto,cto->nc', backward_patches, kernel, precision=lax.Precisi...  17 us
    dot_general x1, matrix products, per_device(): jnp.einsum('ntc,cto->no', forward_patches, kernel, precision=lax.Precisio...  14.5 us
    dot_general x1, matrix products, per_device(): jnp.einsum('ntc,no->cto', forward_patches, flat_up, precision=lax.Precisi...  13.6 us
    ppermute x3, starting transfers between devices, padded_2(): after = lax.ppermute(initial, axis, down)  7.42 us
  transfers between devices with their start and end apart: 8, of which 5 were waited for; matrix products, arithmetic and copies ran while one was open for 19% of the time, Pallas kernels for 0%

profile of v1, /device:TPU:2, one launch (start us, length us, event | category | flops | bytes accessed | tf_op | source)
XLA Modules:
  0.0 354.1 jit_solution(11581929547462301850)
XLA Ops:
  7.2 1.0 pad_maximum_fusion.9
  8.2 2.0 collective-permute-start
  10.2 4.0 %collective-permute-start.1 = (f32[2,1,8,8,256]{4,3,2,1,0:T(8,128)S(1)}, f32[2,1,8,8,256]{4,3,2,1,0:T(8,128)S(1)}, u32[]{:S(2)}, u32[]{:S(2)}) collective-permute-start(f32[2,1,8,8,256]{4,3,2,1,0:T(8,128)S(1)} %get-tuple-element.66), channel_id=1, source_target_pairs={{32,0},{64,32},{96,64},{128,96},{160,128},{192,160},{224,192},{0,2... | collective-permute-start | bytes 393224 | tf_op jit(solution)/shard_map/ppermute | solution.py:16
  14.3 3.4 collective-permute-done
  17.7 0.8 pad_maximum_fusion.19
  18.5 1.7 collective-permute-start.2
  20.2 1.7 collective-permute-start.3
  21.8 1.3 pad_maximum_fusion.2
  23.1 1.3 collective-permute-done.2
  24.8 1.4 pad_maximum_fusion.10
  26.2 1.7 collective-permute-start.5
  27.9 1.4 pad_maximum_fusion.1
  29.3 1.2 fusion.2
  31.2 1.3 fusion.1
  32.5 1.3 fusion
  34.5 2.9 copy-done
  37.5 13.6 %multiply_bitcast_fusion = f32[256,27,256]{2,0,1:T(8,128)} fusion(f32[256,27,256]{2,0,1:T(8,128)S(1)} %constant_dynamic-update-slice_fusion, f32[256,256,1]{1,0,2:T(8,128)S(1)} %bitcast.83), kind=kOutput, calls=%fused_computation | convolution fusion | flops 5437587456 | bytes 14417920 | tf_op jit(solution)/shard_map/ntc,no->cto/dot_general | solution.py:71
  51.2 0.7 constant_dynamic-update-slice_fusion.53
  51.9 0.7 constant_dynamic-update-slice_fusion.52
  52.7 0.7 constant_dynamic-update-slice_fusion.51
  53.4 0.7 constant_dynamic-update-slice_fusion.50
  54.1 0.7 constant_dynamic-update-slice_fusion.49
  54.9 0.7 constant_dynamic-update-slice_fusion.48
  55.6 0.7 constant_dynamic-update-slice_fusion.47
  56.3 159.5 %all-reduce.3.cloned.1.call-done = f32[256,27,256]{2,0,1:T(8,128)} async-done(((f32[256,27,256]{2,0,1:T(8,128)}), f32[256,27,256]{2,0,1:T(8,128)}) %all-reduce.3.cloned.1.call-update) | async-done | bytes 7077904 | tf_op jit(solution)/shard_map/psum | solution.py:70
  215.9 1.8 constant_dynamic-update-slice_fusion.46
  217.7 1.7 constant_dynamic-update-slice_fusion.45
  219.4 1.7 constant_dynamic-update-slice_fusion.44
  221.1 1.8 constant_dynamic-update-slice_fusion.43
  222.9 1.7 constant_dynamic-update-slice_fusion.42
  224.5 1.7 constant_dynamic-update-slice_fusion.41
  226.2 0.7 constant_dynamic-update-slice_fusion.40
  226.9 1.7 constant_dynamic-update-slice_fusion.39
  228.6 1.7 constant_dynamic-update-slice_fusion.38
  230.3 1.7 constant_dynamic-update-slice_fusion.37
  232.0 1.7 constant_dynamic-update-slice_fusion.36
  233.7 1.7 constant_dynamic-update-slice_fusion.35
  235.4 1.7 constant_dynamic-update-slice_fusion.34
  237.1 1.7 constant_dynamic-update-slice_fusion.33
  238.8 0.7 constant_dynamic-update-slice_fusion.32
  239.5 0.7 constant_dynamic-update-slice_fusion.31
  240.2 0.7 constant_dynamic-update-slice_fusion.30
  241.7 0.7 constant_dynamic-update-slice_fusion.28
  242.4 0.7 constant_dynamic-update-slice_fusion.27
  243.1 14.5 %fusion.4 = f32[256,256,1]{1,0,2:T(8,128)} fusion(f32[256,27,256]{2,0,1:T(8,128)S(1)} %bitcast.74, f32[256,27,256]{2,0,1:T(8,128)} %param.4), kind=kOutput, calls=%fused_computation.82 | convolution fusion | flops 5435817984 | bytes 14417920 | tf_op jit(solution)/shard_map/ntc,cto->no/dot_general | solution.py:51
  257.6 17.0 %fusion.5 = f32[256,256,1]{1,0,2:T(8,128)} fusion(f32[256,27,256]{2,0,1:T(8,128)} %constant_dynamic-update-slice_fusion.27, f32[256,27,256]{2,0,1:T(8,128)S(1)} %bitcast.76), kind=kOutput, calls=%fused_computation.83 | convolution fusion | flops 5435817984 | bytes 14417920 | tf_op jit(solution)/shard_map/nto,cto->nc/dot_general | solution.py:58
  274.6 70.5 %all-reduce.5.cloned.1.call-done = f32[256,27,256]{2,0,1:T(8,128)} async-done(((f32[256,27,256]{2,0,1:T(8,128)}), f32[256,27,256]{2,0,1:T(8,128)}) %all-reduce.5.cloned.1.call-update) | async-done | bytes 7077904 | tf_op jit(solution)/shard_map/psum | solution.py:69
  345.1 2.2 constant_dynamic-slice_fusion
  (63 shorter events, 2.4 us)
Async XLA Ops:
  7.2 23.3 %copy-start.2 = (f32[4,8,8,256]{3,2,1,0:T(8,128)S(1)}, f32[4,8,8,256]{3,2,1,0:T(8,128)}, u32[]{:S(2)}) copy-start(f32[4,8,8,256]{3,2,1,0:T(8,128)} %param.3) | copy-start | bytes 786436
  7.2 23.3 %copy-start.1 = (f32[4,8,8,256]{3,2,1,0:T(8,128)S(1)}, f32[4,8,8,256]{3,2,1,0:T(8,128)}, u32[]{:S(2)}) copy-start(f32[4,8,8,256]{3,2,1,0:T(8,128)} %param.5) | copy-start | bytes 786436
  7.2 208.6 %all-reduce.3.cloned.1.call-start = ((), (), s32[]{:S(2)}) async-start(), calls=%async_computation | async-start | bytes 14155776 | tf_op jit(solution)/shard_map/psum | solution.py:70
  8.2 9.4 %collective-permute-start = (f32[2,1,8,8,256]{4,3,2,1,0:T(8,128)S(1)}, f32[2,1,8,8,256]{4,3,2,1,0:T(8,128)S(1)}, u32[]{:S(2)}, u32[]{:S(2)}) collective-permute-start(f32[2,1,8,8,256]{4,3,2,1,0:T(8,128)S(1)} %get-tuple-element.65), channel_id=1, source_target_pairs={{0,32},{32,64},{64,96},{96,128},{128,160},{160,192},{192,224},{224... | collective-permute-start | bytes 393224 | tf_op jit(solution)/shard_map/ppermute | solution.py:15
  10.2 7.4 %collective-permute-start.1 = (f32[2,1,8,8,256]{4,3,2,1,0:T(8,128)S(1)}, f32[2,1,8,8,256]{4,3,2,1,0:T(8,128)S(1)}, u32[]{:S(2)}, u32[]{:S(2)}) collective-permute-start(f32[2,1,8,8,256]{4,3,2,1,0:T(8,128)S(1)} %get-tuple-element.66), channel_id=1, source_target_pairs={{32,0},{64,32},{96,64},{128,96},{160,128},{192,160},{224,192},{0,2... | collective-permute-start | bytes 393224 | tf_op jit(solution)/shard_map/ppermute | solution.py:16
  18.5 5.9 %collective-permute-start.2 = (f32[2,6,1,8,256]{4,3,2,1,0:T(8,128)S(1)}, f32[2,6,1,8,256]{4,3,2,1,0:T(8,128)S(1)}, u32[]{:S(2)}, u32[]{:S(2)}) collective-permute-start(f32[2,6,1,8,256]{4,3,2,1,0:T(8,128)S(1)} %get-tuple-element.57), channel_id=1, source_target_pairs={{0,8},{8,16},{16,24},{24,0},{1,9},{9,17},{17,25},{25,1},{2,10},{10... | collective-permute-start | bytes 294920 | tf_op jit(solution)/shard_map/ppermute | solution.py:15
  20.2 4.6 %collective-permute-start.3 = (f32[2,6,1,8,256]{4,3,2,1,0:T(8,128)S(1)}, f32[2,6,1,8,256]{4,3,2,1,0:T(8,128)S(1)}, u32[]{:S(2)}, u32[]{:S(2)}) collective-permute-start(f32[2,6,1,8,256]{4,3,2,1,0:T(8,128)S(1)} %get-tuple-element.58), channel_id=1, source_target_pairs={{8,0},{16,8},{24,16},{0,24},{9,1},{17,9},{25,17},{1,25},{10,2},{18... | collective-permute-start | bytes 294920 | tf_op jit(solution)/shard_map/ppermute | solution.py:16
  26.2 4.3 %collective-permute-start.4 = (f32[2,6,10,1,256]{4,3,2,1,0:T(1,128)S(1)}, f32[2,6,10,1,256]{4,3,2,1,0:T(1,128)S(1)}, u32[]{:S(2)}, u32[]{:S(2)}) collective-permute-start(f32[2,6,10,1,256]{4,3,2,1,0:T(1,128)S(1)} %get-tuple-element.42), channel_id=1, source_target_pairs={{0,1},{1,2},{2,3},{3,4},{4,5},{5,6},{6,7},{7,0},{8,9},{9,10},{10,1... | collective-permute-start | bytes 368648 | tf_op jit(solution)/shard_map/ppermute | solution.py:15
  26.2 4.3 %collective-permute-start.5 = (f32[2,6,10,1,256]{4,3,2,1,0:T(1,128)S(1)}, f32[2,6,10,1,256]{4,3,2,1,0:T(1,128)S(1)}, u32[]{:S(2)}, u32[]{:S(2)}) collective-permute-start(f32[2,6,10,1,256]{4,3,2,1,0:T(1,128)S(1)} %get-tuple-element.41), channel_id=1, source_target_pairs={{1,0},{2,1},{3,2},{4,3},{5,4},{6,5},{7,6},{0,7},{9,8},{10,9},{11,1... | collective-permute-start | bytes 368648 | tf_op jit(solution)/shard_map/ppermute | solution.py:16
  34.5 2.9 copy-start
  51.1 294.0 %all-reduce.5.cloned.1.call-start = ((), (), s32[]{:S(2)}) async-start(), calls=%async_computation.1 | async-start | bytes 14155776 | tf_op jit(solution)/shard_map/psum | solution.py:69
  215.8 27.3 %slice-start = ((s8[7077888]{0:T(1024)(128)(4,1)}), s8[2883584]{0:T(1024)(128)(4,1)S(1)}, s32[]{:S(2)}) async-start(s8[7077888]{0:T(1024)(128)(4,1)} %bitcast.73), calls=%async_computation.2 | async-start | bytes 5767168
  215.8 23.0 %copy-start.5 = (f32[1,4,8,8,256]{4,3,2,1,0:T(8,128)S(1)}, f32[1,4,8,8,256]{4,3,2,1,0:T(8,128)}, u32[]{:S(2)}) copy-start(f32[1,4,8,8,256]{4,3,2,1,0:T(8,128)} %get-tuple-element.22) | copy-start | bytes 786436
  215.8 24.4 %copy-start.7 = (f32[1,4,8,8,256]{4,3,2,1,0:T(8,128)S(1)}, f32[1,4,8,8,256]{4,3,2,1,0:T(8,128)}, u32[]{:S(2)}) copy-start(f32[1,4,8,8,256]{4,3,2,1,0:T(8,128)} %get-tuple-element.4) | copy-start | bytes 786436
  215.8 25.1 %copy-start.4 = (f32[1,4,8,8,256]{4,3,2,1,0:T(8,128)S(1)}, f32[1,4,8,8,256]{4,3,2,1,0:T(8,128)}, u32[]{:S(2)}) copy-start(f32[1,4,8,8,256]{4,3,2,1,0:T(8,128)} %get-tuple-element.21) | copy-start | bytes 786436
  215.8 25.8 %copy-start.3 = (f32[1,4,8,8,256]{4,3,2,1,0:T(8,128)S(1)}, f32[1,4,8,8,256]{4,3,2,1,0:T(8,128)}, u32[]{:S(2)}) copy-start(f32[1,4,8,8,256]{4,3,2,1,0:T(8,128)} %get-tuple-element.43) | copy-start | bytes 786436
  215.9 26.6 %copy-start.6 = (f32[1,4,8,8,256]{4,3,2,1,0:T(8,128)S(1)}, f32[1,4,8,8,256]{4,3,2,1,0:T(8,128)}, u32[]{:S(2)}) copy-start(f32[1,4,8,8,256]{4,3,2,1,0:T(8,128)} %get-tuple-element.3) | copy-start | bytes 786436
  221.1 22.1 %slice-start.1 = ((s8[7077888]{0:T(1024)(128)(4,1)}), s8[4194304]{0:T(1024)(128)(4,1)S(1)}, s32[]{:S(2)}) async-start(s8[7077888]{0:T(1024)(128)(4,1)} %bitcast.73), calls=%async_computation.3 | async-start | bytes 8388608
  241.0 16.7 %slice-start.2 = ((s8[7077888]{0:T(1024)(128)(4,1)}), s8[4194304]{0:T(1024)(128)(4,1)S(1)}, s32[]{:S(2)}) async-start(s8[7077888]{0:T(1024)(128)(4,1)} %bitcast.75), calls=%async_computation.4 | async-start | bytes 8388608
  243.1 14.5 %slice-start.3 = ((s8[7077888]{0:T(1024)(128)(4,1)}), s8[2883584]{0:T(1024)(128)(4,1)S(1)}, s32[]{:S(2)}) async-start(s8[7077888]{0:T(1024)(128)(4,1)} %bitcast.75), calls=%async_computation.5 | async-start | bytes 5767168
Sparse Core Ops, SparseCore 0:
  51.3 164.4 all-reduce.2
  219.3 125.8 all-reduce.4
